TPU v7x, 32 devices: a whole 2x2x4 slice. The times are simulated.
32 devices in a mesh: tiles: 2 (over x), space: 8 (over z, y), chan: 2 (over core).
Axes of the slice: x: 2, y: 2, z: 4, core: 2. Of those that a mesh axis runs over, the one named last changes fastest.
Arguments:
- volume: bfloat16 [32, 64, 32, 256], P(None, 'space', 'tiles', 'chan'), parts along dimension 2, may hold values from -6 to 6
- weight_one: bfloat16 [3, 3, 3, 256, 256], replicated, may hold values from -0.078125 to 0.078125
- bias_one: float32 [256], replicated, may hold values from -3 to 3
- weight_two: bfloat16 [3, 3, 3, 256, 256], replicated, may hold values from -0.078125 to 0.078125
- bias_two: float32 [256], replicated, may hold values from -3 to 3
Outputs:
- features: bfloat16 [32, 64, 32, 256], P('space', None, 'tiles', 'chan'), parts along dimension 2
There are 2 independent parts, one for each index of `tiles`. A program takes and returns all parts, laid end to end along the dimension named above; an argument that names none is the same for every part. Nothing has to cross between parts.
All inputs are finite; a program needn't handle non-finite values.
Results may differ from a plain program's by a relative error of at most 0.0044.
Values may be sent and summed in bfloat16 or wider, within the bound.
A program may use at most 128 MiB of HBM per device.

v0:
```python
import jax
import jax.numpy as jnp
from jax import lax
from jax.sharding import PartitionSpec as P


def padded(x, sides, width):
    for axis, dim in sides:
        devices, length = (lax.axis_size(axis), x.shape[dim])
        up = [(i, (i + 1) % devices) for i in range(devices - 1)]
        down = [(j, i) for i, j in up]
        last = lax.slice_in_dim(x, length - width, length, axis=dim)
        first = lax.slice_in_dim(x, 0, width, axis=dim)
        before = lax.ppermute(last, axis, up)
        after = lax.ppermute(first, axis, down)
        x = jnp.concatenate([before, x, after], axis=dim)
    return x


def convolve(field, kernel):
    return lax.conv_general_dilated(
        field[None],
        kernel,
        (1, 1, 1),
        ((0, 0), (1, 1), (1, 1)),
        dimension_numbers=("NDHWC", "DHWIO", "NDHWC"),
        preferred_element_type=jnp.float32,
    )[0]


def pad_layer(field):
    return padded(field, (("space", 0),), 1)


def body(volume, weight_one, bias_one, weight_two, bias_two):
    slab_data = lax.all_to_all(volume, "space", split_axis=0, concat_axis=1, tiled=True)
    share = slab_data.shape[3]
    offset = lax.axis_index("chan") * share

    def layer(field, kernel, bias):
        part_kernel = lax.dynamic_slice_in_dim(kernel, offset, share, 3)
        summed = lax.psum_scatter(
            convolve(field, part_kernel), "chan", scatter_dimension=3, tiled=True
        )
        return summed + lax.dynamic_slice_in_dim(bias, offset, share, 0)

    hidden = jnp.maximum(layer(pad_layer(slab_data), weight_one, bias_one), 0.0).astype(
        jnp.bfloat16
    )
    result = layer(pad_layer(hidden), weight_two, bias_two)
    return jnp.maximum(result, 0.0).astype(jnp.bfloat16)


def solution(mesh):
    return jax.shard_map(
        body,
        mesh=mesh,
        in_specs=(P(None, "space", "tiles", "chan"), P(), P(), P(), P()),
        out_specs=P("space", None, "tiles", "chan"),
        check_vma=False,
    )
```

profile of v0, /device:TPU:0, one launch (start us, length us, event | category | flops | bytes accessed | tf_op | source)
XLA Modules:
  0.0 152.2 jit_solution(18392344283605213715)
XLA Ops:
  6.5 0.0 copy-start
  6.5 0.0 reduce-scatter.3.cloned.1.call-start
  6.5 33.3 %all_to_all.18 = bf16[32,8,16,128]{3,2,1,0:T(8,128)(2,1)S(1)} all-to-all(bf16[32,8,16,128]{3,2,1,0:T(8,128)(2,1)} %param.5), channel_id=1, replica_groups=mesh['tiles'=2,'space'=8,'chan'=2] {'space'}, dimensions={0} | all-to-all | bytes 2097152 | tf_op jit(solution)/shard_map/all_to_all | solution.py:36
  39.9 0.0 copy-start.2
  39.9 1.0 copy-done.2
  40.8 0.8 fusion.33
  41.7 4.1 %collective-permute-start = (bf16[1,64,16,128]{3,2,1,0:T(8,128)(2,1)}, bf16[1,64,16,128]{3,2,1,0:T(8,128)(2,1)}, u32[]{:S(2)}, u32[]{:S(2)}) collective-permute-start(bf16[1,64,16,128]{3,2,1,0:T(8,128)(2,1)} %bitcast.2), channel_id=1, source_target_pairs={{0,2},{2,4},{4,6},{6,8},{8,10},{10,12},{12,14},{1,3},{3,5},{5,7},{... | collective-permute-start | bytes 786440 | tf_op jit(solution)/shard_map/ppermute | solution.py:14
  45.7 1.3 collective-permute-start.1
  47.0 1.4 copy.14
  48.4 6.9 %collective-permute-done = bf16[1,64,16,128]{3,2,1,0:T(8,128)(2,1)} collective-permute-done((bf16[1,64,16,128]{3,2,1,0:T(8,128)(2,1)}, bf16[1,64,16,128]{3,2,1,0:T(8,128)(2,1)}, u32[]{:S(2)}, u32[]{:S(2)}) %collective-permute-start) | collective-permute-done | bytes 262176 | tf_op jit(solution)/shard_map/ppermute | solution.py:14
  55.4 0.0 collective-permute-done.1
  55.4 1.2 maximum_bitcast_fusion
  56.6 0.4 copy.23
  57.0 0.4 pad.clone
  57.4 1.5 %copy.17 = bf16[6,64,1,8,3,128]{5,3,4,1,0,2:T(8,128)(2,1)S(1)} copy(bf16[6,64,1,8,3,128]{5,1,4,3,0,2:T(8,128)(2,1)S(1)} %bitcast.31) | data formatting | bytes 4718592 | tf_op jit(solution)/shard_map/conv_general_dilated | solution.py:21
  58.9 0.0 copy-start.6
  58.9 0.4 slice.30
  59.4 0.0 copy-done
  59.4 0.2 copy-done.6
  59.6 13.5 %broadcast_select_fusion.1 = f32[4,64,8,3,256]{4,2,3,1,0:T(8,128)S(1)} fusion(pred[8,3]{0,1:T(4,128)(4,1)S(1)} %copy-done.6, bf16[6,64,1,7,2,128]{5,3,4,1,0,2:T(8,128)(2,1)S(1)} %slice.30, bf16[6,64,1,8,3,128]{5,3,4,1,0,2:T(8,128)(2,1)S(1)} %copy.17, bf16[3,3,3,256,256]{4,3,2,1,0:T(8,128)(2,1)S(1)} %copy-done, s32[]{:T(128)S(6)} %select_n.2), kind=kOutput, calls=%fused_computation.18 | convolution fusion | flops 10771759104 | bytes 11993604 | tf_op jit(solution)/shard_map/conv_general_dilated | solution.py:21
  73.0 1.9 %copy.18 = f32[4,64,8,3,256]{4,1,3,2,0:T(8,128)S(1)} copy(f32[4,64,8,3,256]{4,2,3,1,0:T(8,128)S(1)} %broadcast_select_fusion.1) | data formatting | bytes 12582912 | tf_op jit(solution)/shard_map/conv_general_dilated | solution.py:21
  75.0 2.4 %slice_bitcast_fusion.1 = f32[4,64,16,256]{3,1,2,0:T(8,128)} fusion(f32[4,64,1,24,256]{4,1,3,0,2:T(8,128)S(1)} %bitcast.28), kind=kLoop, calls=%fused_computation.4 | loop fusion | bytes 8388608 | tf_op jit(solution)/shard_map/squeeze | solution.py:21
  77.4 0.0 copy-start.4
  77.4 0.0 reduce-scatter.3.cloned.1.call-update
  77.4 0.0 reduce-scatter.5.cloned.1.call-start
  77.5 0.6 copy-done.4
  78.1 0.1 dynamic_slice.13
  78.2 11.9 %reduce-scatter.3.cloned.1.call-done = f32[4,64,16,128]{3,1,2,0:T(8,128)} async-done(((f32[4,64,16,256]{3,1,2,0:T(8,128)}), f32[4,64,16,128]{3,1,2,0:T(8,128)}) %reduce-scatter.3.cloned.1.call-update) | async-done | bytes 2097168 | tf_op jit(solution)/shard_map/reduce_scatter | solution.py:42
  90.1 1.9 %maximum_convert_fusion.1 = bf16[4,64,16,128]{3,1,2,0:T(8,128)(2,1)S(1)} fusion(f32[4,64,16,128]{3,1,2,0:T(8,128)} %reduce-scatter.3.cloned.1.call-done, f32[128]{0:T(128)S(1)} %dynamic_slice.13), kind=kLoop, calls=%fused_computation.20 | loop fusion | flops 1572864 | bytes 3146240 | tf_op jit(solution)/shard_map/convert_element_type | solution.py:47
  92.0 3.8 %collective-permute-start.2 = (bf16[1,64,16,128]{3,1,2,0:T(8,128)(2,1)S(1)}, bf16[1,64,16,128]{3,1,2,0:T(8,128)(2,1)S(1)}, u32[]{:S(2)}, u32[]{:S(2)}) collective-permute-start(bf16[1,64,16,128]{3,1,2,0:T(8,128)(2,1)S(1)} %get-tuple-element.5), channel_id=1, source_target_pairs={{0,2},{2,4},{4,6},{6,8},{8,10},{10,12},{12,14},{1,3},{3,5},{5,7},{... | collective-permute-start | bytes 786440 | tf_op jit(solution)/shard_map/ppermute | solution.py:14
  95.8 1.5 collective-permute-start.3
  97.2 10.0 %collective-permute-done.2 = bf16[1,64,16,128]{3,1,2,0:T(8,128)(2,1)S(1)} collective-permute-done((bf16[1,64,16,128]{3,1,2,0:T(8,128)(2,1)S(1)}, bf16[1,64,16,128]{3,1,2,0:T(8,128)(2,1)S(1)}, u32[]{:S(2)}, u32[]{:S(2)}) %collective-permute-start.2) | collective-permute-done | bytes 262176 | tf_op jit(solution)/shard_map/ppermute | solution.py:14
  107.3 0.0 collective-permute-done.3
  107.3 0.2 maximum_bitcast_fusion.1
  107.5 0.4 pad.2
  107.8 0.0 copy-start.3
  107.9 1.5 %copy.20 = bf16[6,64,1,8,3,128]{5,3,4,1,0,2:T(8,128)(2,1)S(1)} copy(bf16[6,64,1,8,3,128]{5,1,4,3,0,2:T(8,128)(2,1)S(1)} %bitcast.30) | data formatting | bytes 4718592 | tf_op jit(solution)/shard_map/conv_general_dilated | solution.py:21
  109.4 0.4 slice.34
  109.8 0.0 copy-done.3
  109.9 13.5 %broadcast_select_fusion = f32[4,64,8,3,256]{4,2,3,1,0:T(8,128)S(1)} fusion(pred[8,3]{0,1:T(4,128)(4,1)S(1)} %copy-done.6, bf16[6,64,1,7,2,128]{5,3,4,1,0,2:T(8,128)(2,1)S(1)} %slice.34, bf16[6,64,1,8,3,128]{5,3,4,1,0,2:T(8,128)(2,1)S(1)} %copy.20, bf16[3,3,3,256,256]{4,3,2,1,0:T(8,128)(2,1)S(1)} %copy-done.3, s32[]{:T(128)S(6)} %select_n.2), kind=kOutput, calls=%fused_computation.17 | convolution fusion | flops 10771759104 | bytes 11993604 | tf_op jit(solution)/shard_map/conv_general_dilated | solution.py:21
  123.3 1.9 %copy.21 = f32[4,64,8,3,256]{4,1,3,2,0:T(8,128)S(1)} copy(f32[4,64,8,3,256]{4,2,3,1,0:T(8,128)S(1)} %broadcast_select_fusion) | data formatting | bytes 12582912 | tf_op jit(solution)/shard_map/conv_general_dilated | solution.py:21
  125.3 2.4 %slice_bitcast_fusion = f32[4,64,16,256]{3,1,2,0:T(8,128)} fusion(f32[4,64,1,24,256]{4,1,3,0,2:T(8,128)S(1)} %bitcast.29), kind=kLoop, calls=%fused_computation.3 | loop fusion | bytes 8388608 | tf_op jit(solution)/shard_map/squeeze | solution.py:21
  127.7 0.0 copy-start.5
  127.7 0.0 reduce-scatter.5.cloned.1.call-update
  127.8 0.7 copy-done.5
  128.4 0.0 copy-start.1
  128.4 0.1 dynamic_slice.15
  128.5 13.4 %reduce-scatter.5.cloned.1.call-done = f32[4,64,16,128]{3,1,2,0:T(8,128)} async-done(((f32[4,64,16,256]{3,1,2,0:T(8,128)}), f32[4,64,16,128]{3,1,2,0:T(8,128)}) %reduce-scatter.5.cloned.1.call-update) | async-done | bytes 2097168 | tf_op jit(solution)/shard_map/reduce_scatter | solution.py:42
  141.8 1.9 %maximum_convert_fusion = bf16[4,64,16,128]{3,1,2,0:T(8,128)(2,1)S(1)} fusion(f32[4,64,16,128]{3,1,2,0:T(8,128)} %reduce-scatter.5.cloned.1.call-done, f32[128]{0:T(128)S(1)} %dynamic_slice.15), kind=kLoop, calls=%fused_computation.19 | loop fusion | flops 1572864 | bytes 3146240 | tf_op jit(solution)/shard_map/convert_element_type | solution.py:51
  143.7 1.7 %copy.22 = bf16[4,64,16,128]{3,2,1,0:T(8,128)(2,1)} copy(bf16[4,64,16,128]{3,1,2,0:T(8,128)(2,1)S(1)} %maximum_convert_fusion) | data formatting | bytes 2097152 | tf_op jit(solution)/shard_map/convert_element_type | solution.py:51
  145.4 0.0 copy-done.1
  (1 shorter events, 0.0 us)
Async XLA Ops:
  6.5 52.8 %copy-start = (bf16[3,3,3,256,256]{4,3,2,1,0:T(8,128)(2,1)S(1)}, bf16[3,3,3,256,256]{4,3,2,1,0:T(8,128)(2,1)}, u32[]{:S(2)}) copy-start(bf16[3,3,3,256,256]{4,3,2,1,0:T(8,128)(2,1)} %param.6) | copy-start | bytes 10616836
  6.5 83.5 %reduce-scatter.3.cloned.1.call-start = ((), (), s32[]{:S(2)}) async-start(), calls=%async_computation.3 | async-start | bytes 6291456 | tf_op jit(solution)/shard_map/reduce_scatter | solution.py:42
  39.9 1.0 copy-start.2
  41.7 13.7 %collective-permute-start = (bf16[1,64,16,128]{3,2,1,0:T(8,128)(2,1)}, bf16[1,64,16,128]{3,2,1,0:T(8,128)(2,1)}, u32[]{:S(2)}, u32[]{:S(2)}) collective-permute-start(bf16[1,64,16,128]{3,2,1,0:T(8,128)(2,1)} %bitcast.2), channel_id=1, source_target_pairs={{0,2},{2,4},{4,6},{6,8},{8,10},{10,12},{12,14},{1,3},{3,5},{5,7},{... | collective-permute-start | bytes 786440 | tf_op jit(solution)/shard_map/ppermute | solution.py:14
  45.7 9.6 %collective-permute-start.1 = (bf16[1,64,16,128]{3,2,1,0:T(8,128)(2,1)}, bf16[1,64,16,128]{3,2,1,0:T(8,128)(2,1)}, u32[]{:S(2)}, u32[]{:S(2)}) collective-permute-start(bf16[1,64,16,128]{3,2,1,0:T(8,128)(2,1)} %bitcast.5), channel_id=1, source_target_pairs={{2,0},{4,2},{6,4},{8,6},{10,8},{12,10},{14,12},{3,1},{5,3},{7,5},{... | collective-permute-start | bytes 786440 | tf_op jit(solution)/shard_map/ppermute | solution.py:15
  58.9 0.7 copy-start.6
  77.4 0.7 copy-start.4
  77.4 64.4 %reduce-scatter.5.cloned.1.call-start = ((), (), s32[]{:S(2)}) async-start(), calls=%async_computation.4 | async-start | bytes 6291456 | tf_op jit(solution)/shard_map/reduce_scatter | solution.py:42
  92.0 15.3 %collective-permute-start.2 = (bf16[1,64,16,128]{3,1,2,0:T(8,128)(2,1)S(1)}, bf16[1,64,16,128]{3,1,2,0:T(8,128)(2,1)S(1)}, u32[]{:S(2)}, u32[]{:S(2)}) collective-permute-start(bf16[1,64,16,128]{3,1,2,0:T(8,128)(2,1)S(1)} %get-tuple-element.5), channel_id=1, source_target_pairs={{0,2},{2,4},{4,6},{6,8},{8,10},{10,12},{12,14},{1,3},{3,5},{5,7},{... | collective-permute-start | bytes 786440 | tf_op jit(solution)/shard_map/ppermute | solution.py:14
  95.8 11.5 %collective-permute-start.3 = (bf16[1,64,16,128]{3,1,2,0:T(8,128)(2,1)S(1)}, bf16[1,64,16,128]{3,1,2,0:T(8,128)(2,1)S(1)}, u32[]{:S(2)}, u32[]{:S(2)}) collective-permute-start(bf16[1,64,16,128]{3,1,2,0:T(8,128)(2,1)S(1)} %get-tuple-element.6), channel_id=1, source_target_pairs={{2,0},{4,2},{6,4},{8,6},{10,8},{12,10},{14,12},{3,1},{5,3},{7,5},{... | collective-permute-start | bytes 786440 | tf_op jit(solution)/shard_map/ppermute | solution.py:15
  107.8 2.0 %copy-start.3 = (bf16[3,3,3,256,256]{4,3,2,1,0:T(8,128)(2,1)S(1)}, bf16[3,3,3,256,256]{4,3,2,1,0:T(8,128)(2,1)}, u32[]{:S(2)}) copy-start(bf16[3,3,3,256,256]{4,3,2,1,0:T(8,128)(2,1)} %param.8) | copy-start | bytes 10616836
  127.7 0.7 copy-start.5
  128.4 17.0 %copy-start.1 = (bf16[3,3,3,256,256]{4,3,2,1,0:T(8,128)(2,1)S(1)}, bf16[3,3,3,256,256]{4,3,2,1,0:T(8,128)(2,1)}, u32[]{:S(2)}) copy-start(bf16[3,3,3,256,256]{4,3,2,1,0:T(8,128)(2,1)} %param.6) | copy-start | bytes 10616836
Sparse Core Ops, SparseCore 0:
  77.6 12.4 reduce-scatter.2
  127.9 13.9 reduce-scatter.4
where the time goes:
time: 153 us; the launch traced here: 152 us
  waiting for transfers between devices  42.2 us (28%)
  blocking collectives  33.3 us (22%)
  matrix products  26.9 us (18%)
  local copies, waits for them, and re-layouts  20.4 us (13%)
  between operations  13.6 us (9%)
  starting transfers between devices  10.6 us (7%)
  other arithmetic  5.18 us (3%)
    all_to_all x1, blocking collectives, body(): lax.all_to_all(volume, 'space', split_axis=0, concat_axis=1, tiled=True)  33.3 us
    conv_general_dilated x2, matrix products, convolve(): lax.conv_general_dilated(field[None], kernel, (1, 1, 1), ((0, 0), (1, 1),...  26.9 us
    reduce_scatter x2, waiting for transfers between devices, layer(): lax.psum_scatter(convolve(field, part_kernel), 'chan', scatter_dimension=...  25.3 us
    ppermute x2, waiting for transfers between devices, padded(): before = lax.ppermute(last, axis, up)  17 us
    ppermute x2, starting transfers between devices, padded(): before = lax.ppermute(last, axis, up)  7.83 us
    conv_general_dilated x6, local copies, waits for them, and re-layouts, convolve(): lax.conv_general_dilated(field[None], kernel, (1, 1, 1), ((0, 0), (1, 1),...  7.73 us
    squeeze x2, local copies, waits for them, and re-layouts, convolve(): lax.conv_general_dilated(field[None], kernel, (1, 1, 1), ((0, 0), (1, 1),...  4.89 us
  transfers between devices with their start and end apart: 6, of which 4 were waited for; matrix products, arithmetic and copies ran while one was open for 1% of the time, Pallas kernels for 0%

commit v1 on v0

--- a/solution.py
+++ b/solution.py
@@ -33,7 +33,10 @@
 
 
 def body(volume, weight_one, bias_one, weight_two, bias_two):
-    slab_data = lax.all_to_all(volume, "space", split_axis=0, concat_axis=1, tiled=True)
+    slab_data = jnp.concatenate(
+        lax.all_to_all(jnp.stack(jnp.split(volume, lax.axis_size("space"), axis=0)), "space", 0, 0),
+        axis=1,
+    )
     share = slab_data.shape[3]
     offset = lax.axis_index("chan") * share
 

time: 153 us -> 160 us (1.046)
  local copies, waits for them, and re-layouts: 20.4 us -> 26.8 us
    unnamed x15 -> x22, local copies, waits for them, and re-layouts: 2.91 us -> 9.58 us
  transfers between devices with their start and end apart: 6 -> 6, of which waited for: 4 -> 4; matrix products, arithmetic and copies ran while one was open for 1% -> 0% of each run, Pallas kernels for 0% -> 0%
where the time goes in v1:
time: 160 us
  waiting for transfers between devices  43.6 us (27%)
  blocking collectives  32.8 us (20%)
  matrix products  26.9 us (17%)
  local copies, waits for them, and re-layouts  26.8 us (17%)
  between operations  13.6 us (8%)
  starting transfers between devices  10.6 us (7%)
  other arithmetic  5.49 us (3%)
    all_to_all x1, blocking collectives, body(): lax.all_to_all(jnp.stack(jnp.split(volume, lax.axis_size('space'), axis=0...  32.8 us
    conv_general_dilated x2, matrix products, convolve(): lax.conv_general_dilated(field[None], kernel, (1, 1, 1), ((0, 0), (1, 1),...  26.9 us
    reduce_scatter x2, waiting for transfers between devices, layer(): lax.psum_scatter(convolve(field, part_kernel), 'chan', scatter_dimension=...  25.2 us
    ppermute x2, waiting for transfers between devices, padded(): before = lax.ppermute(last, axis, up)  18.4 us
    unnamed x22, local copies, waits for them, and re-layouts  9.58 us
    ppermute x2, starting transfers between devices, padded(): before = lax.ppermute(last, axis, up)  7.83 us
    conv_general_dilated x6, local copies, waits for them, and re-layouts, convolve(): lax.conv_general_dilated(field[None], kernel, (1, 1, 1), ((0, 0), (1, 1),...  7.73 us
    squeeze x2, local copies, waits for them, and re-layouts, convolve(): lax.conv_general_dilated(field[None], kernel, (1, 1, 1), ((0, 0), (1, 1),...  4.89 us
  transfers between devices with their start and end apart: 6, of which 4 were waited for; matrix products, arithmetic and copies ran while one was open for 0% of the time, Pallas kernels for 0%

profile of v1, /device:TPU:0, one launch (start us, length us, event | category | flops | bytes accessed | tf_op | source)
XLA Modules:
  0.0 160.0 jit_solution(14186295855541255679)
XLA Ops:
  6.5 0.0 copy-start
  6.5 0.0 reduce-scatter.3.cloned.1.call-start
  6.5 1.1 bitcast_dynamic-update-slice_fusion.7
  7.6 1.0 bitcast_dynamic-update-slice_fusion.6
  8.6 0.9 bitcast_dynamic-update-slice_fusion.5
  9.5 0.9 bitcast_dynamic-update-slice_fusion.4
  10.4 0.9 bitcast_dynamic-update-slice_fusion.3
  11.4 0.9 bitcast_dynamic-update-slice_fusion.2
  12.3 0.9 bitcast_dynamic-update-slice_fusion.1
  13.2 0.9 bitcast_dynamic-update-slice_fusion
  14.2 32.8 %all_to_all.5 = bf16[8,4,8,16,128]{4,3,2,1,0:T(8,128)(2,1)S(1)} all-to-all(bf16[8,4,8,16,128]{4,3,2,1,0:T(8,128)(2,1)S(1)} %bitcast_dynamic-update-slice_fusion), channel_id=1, replica_groups=mesh['tiles'=2,'space'=8,'chan'=2] {'space'}, dimensions={0} | all-to-all | bytes 2097152 | tf_op jit(solution)/shard_map/all_to_all | solution.py:37
  47.0 0.3 copy.26
  47.3 0.0 copy-start.2
  47.3 1.0 copy-done.2
  48.3 0.8 fusion.33
  49.1 4.1 %collective-permute-start = (bf16[1,64,16,128]{3,2,1,0:T(8,128)(2,1)}, bf16[1,64,16,128]{3,2,1,0:T(8,128)(2,1)}, u32[]{:S(2)}, u32[]{:S(2)}) collective-permute-start(bf16[1,64,16,128]{3,2,1,0:T(8,128)(2,1)} %bitcast.9), channel_id=1, source_target_pairs={{0,2},{2,4},{4,6},{6,8},{8,10},{10,12},{12,14},{1,3},{3,5},{5,7},{... | collective-permute-start | bytes 786440 | tf_op jit(solution)/shard_map/ppermute | solution.py:14
  53.2 1.3 collective-permute-start.1
  54.5 8.3 %collective-permute-done = bf16[1,64,16,128]{3,2,1,0:T(8,128)(2,1)} collective-permute-done((bf16[1,64,16,128]{3,2,1,0:T(8,128)(2,1)}, bf16[1,64,16,128]{3,2,1,0:T(8,128)(2,1)}, u32[]{:S(2)}, u32[]{:S(2)}) %collective-permute-start) | collective-permute-done | bytes 262176 | tf_op jit(solution)/shard_map/ppermute | solution.py:14
  62.8 0.0 collective-permute-done.1
  62.8 1.5 maximum_bitcast_fusion
  64.4 0.4 copy.23
  64.8 0.4 pad.clone
  65.2 1.5 copy.17
  66.7 0.0 copy-start.6
  66.7 0.4 slice.30
  67.1 0.0 copy-done
  67.1 0.2 copy-done.6
  67.4 13.5 %broadcast_select_fusion.1 = f32[4,64,8,3,256]{4,2,3,1,0:T(8,128)S(1)} fusion(pred[8,3]{0,1:T(4,128)(4,1)S(1)} %copy-done.6, bf16[6,64,1,7,2,128]{5,3,4,1,0,2:T(8,128)(2,1)S(1)} %slice.30, bf16[6,64,1,8,3,128]{5,3,4,1,0,2:T(8,128)(2,1)S(1)} %copy.17, bf16[3,3,3,256,256]{4,3,2,1,0:T(8,128)(2,1)S(1)} %copy-done, s32[]{:T(128)S(6)} %select_n.2), kind=kOutput, calls=%fused_computation.18 | convolution fusion | flops 10771759104 | bytes 11993604 | tf_op jit(solution)/shard_map/conv_general_dilated | solution.py:21
  80.8 1.9 %copy.18 = f32[4,64,8,3,256]{4,1,3,2,0:T(8,128)S(1)} copy(f32[4,64,8,3,256]{4,2,3,1,0:T(8,128)S(1)} %broadcast_select_fusion.1) | data formatting | bytes 12582912 | tf_op jit(solution)/shard_map/conv_general_dilated | solution.py:21
  82.7 2.4 %slice_bitcast_fusion.1 = f32[4,64,16,256]{3,1,2,0:T(8,128)} fusion(f32[4,64,1,24,256]{4,1,3,0,2:T(8,128)S(1)} %bitcast.44), kind=kLoop, calls=%fused_computation.4 | loop fusion | bytes 8388608 | tf_op jit(solution)/shard_map/squeeze | solution.py:21
  85.2 0.0 copy-start.4
  85.2 0.0 reduce-scatter.3.cloned.1.call-update
  85.2 0.0 reduce-scatter.5.cloned.1.call-start
  85.3 0.6 copy-done.4
  85.9 0.1 dynamic_slice.13
  85.9 11.9 %reduce-scatter.3.cloned.1.call-done = f32[4,64,16,128]{3,1,2,0:T(8,128)} async-done(((f32[4,64,16,256]{3,1,2,0:T(8,128)}), f32[4,64,16,128]{3,1,2,0:T(8,128)}) %reduce-scatter.3.cloned.1.call-update) | async-done | bytes 2097168 | tf_op jit(solution)/shard_map/reduce_scatter | solution.py:45
  97.8 1.9 %maximum_convert_fusion.1 = bf16[4,64,16,128]{3,1,2,0:T(8,128)(2,1)S(1)} fusion(f32[4,64,16,128]{3,1,2,0:T(8,128)} %reduce-scatter.3.cloned.1.call-done, f32[128]{0:T(128)S(1)} %dynamic_slice.13), kind=kLoop, calls=%fused_computation.20 | loop fusion | flops 1572864 | bytes 3146240 | tf_op jit(solution)/shard_map/convert_element_type | solution.py:50
  99.8 3.8 %collective-permute-start.2 = (bf16[1,64,16,128]{3,1,2,0:T(8,128)(2,1)S(1)}, bf16[1,64,16,128]{3,1,2,0:T(8,128)(2,1)S(1)}, u32[]{:S(2)}, u32[]{:S(2)}) collective-permute-start(bf16[1,64,16,128]{3,1,2,0:T(8,128)(2,1)S(1)} %get-tuple-element.5), channel_id=1, source_target_pairs={{0,2},{2,4},{4,6},{6,8},{8,10},{10,12},{12,14},{1,3},{3,5},{5,7},{... | collective-permute-start | bytes 786440 | tf_op jit(solution)/shard_map/ppermute | solution.py:14
  103.5 1.5 collective-permute-start.3
  105.0 10.0 %collective-permute-done.2 = bf16[1,64,16,128]{3,1,2,0:T(8,128)(2,1)S(1)} collective-permute-done((bf16[1,64,16,128]{3,1,2,0:T(8,128)(2,1)S(1)}, bf16[1,64,16,128]{3,1,2,0:T(8,128)(2,1)S(1)}, u32[]{:S(2)}, u32[]{:S(2)}) %collective-permute-start.2) | collective-permute-done | bytes 262176 | tf_op jit(solution)/shard_map/ppermute | solution.py:14
  115.0 0.0 collective-permute-done.3
  115.0 0.2 maximum_bitcast_fusion.1
  115.2 0.4 pad.2
  115.6 0.0 copy-start.3
  115.6 1.5 copy.20
  117.2 0.4 slice.34
  117.6 0.0 copy-done.3
  117.6 13.5 %broadcast_select_fusion = f32[4,64,8,3,256]{4,2,3,1,0:T(8,128)S(1)} fusion(pred[8,3]{0,1:T(4,128)(4,1)S(1)} %copy-done.6, bf16[6,64,1,7,2,128]{5,3,4,1,0,2:T(8,128)(2,1)S(1)} %slice.34, bf16[6,64,1,8,3,128]{5,3,4,1,0,2:T(8,128)(2,1)S(1)} %copy.20, bf16[3,3,3,256,256]{4,3,2,1,0:T(8,128)(2,1)S(1)} %copy-done.3, s32[]{:T(128)S(6)} %select_n.2), kind=kOutput, calls=%fused_computation.17 | convolution fusion | flops 10771759104 | bytes 11993604 | tf_op jit(solution)/shard_map/conv_general_dilated | solution.py:21
  131.1 1.9 %copy.21 = f32[4,64,8,3,256]{4,1,3,2,0:T(8,128)S(1)} copy(f32[4,64,8,3,256]{4,2,3,1,0:T(8,128)S(1)} %broadcast_select_fusion) | data formatting | bytes 12582912 | tf_op jit(solution)/shard_map/conv_general_dilated | solution.py:21
  133.1 2.4 %slice_bitcast_fusion = f32[4,64,16,256]{3,1,2,0:T(8,128)} fusion(f32[4,64,1,24,256]{4,1,3,0,2:T(8,128)S(1)} %bitcast.45), kind=kLoop, calls=%fused_computation.3 | loop fusion | bytes 8388608 | tf_op jit(solution)/shard_map/squeeze | solution.py:21
  135.5 0.0 copy-start.5
  135.5 0.0 reduce-scatter.5.cloned.1.call-update
  135.5 0.7 copy-done.5
  136.2 0.0 copy-start.1
  136.2 0.1 dynamic_slice.15
  136.3 13.3 %reduce-scatter.5.cloned.1.call-done = f32[4,64,16,128]{3,1,2,0:T(8,128)} async-done(((f32[4,64,16,256]{3,1,2,0:T(8,128)}), f32[4,64,16,128]{3,1,2,0:T(8,128)}) %reduce-scatter.5.cloned.1.call-update) | async-done | bytes 2097168 | tf_op jit(solution)/shard_map/reduce_scatter | solution.py:45
  149.6 1.9 %maximum_convert_fusion = bf16[4,64,16,128]{3,1,2,0:T(8,128)(2,1)S(1)} fusion(f32[4,64,16,128]{3,1,2,0:T(8,128)} %reduce-scatter.5.cloned.1.call-done, f32[128]{0:T(128)S(1)} %dynamic_slice.15), kind=kLoop, calls=%fused_computation.19 | loop fusion | flops 1572864 | bytes 3146240 | tf_op jit(solution)/shard_map/convert_element_type | solution.py:54
  151.5 1.7 %copy.22 = bf16[4,64,16,128]{3,2,1,0:T(8,128)(2,1)} copy(bf16[4,64,16,128]{3,1,2,0:T(8,128)(2,1)S(1)} %maximum_convert_fusion) | data formatting | bytes 2097152 | tf_op jit(solution)/shard_map/convert_element_type | solution.py:54
  153.1 0.0 copy-done.1
  (1 shorter events, 0.0 us)
Async XLA Ops:
  6.5 60.6 %copy-start = (bf16[3,3,3,256,256]{4,3,2,1,0:T(8,128)(2,1)S(1)}, bf16[3,3,3,256,256]{4,3,2,1,0:T(8,128)(2,1)}, u32[]{:S(2)}) copy-start(bf16[3,3,3,256,256]{4,3,2,1,0:T(8,128)(2,1)} %param.6) | copy-start | bytes 10616836
  6.5 91.3 %reduce-scatter.3.cloned.1.call-start = ((), (), s32[]{:S(2)}) async-start(), calls=%async_computation.3 | async-start | bytes 6291456 | tf_op jit(solution)/shard_map/reduce_scatter | solution.py:45
  47.3 1.0 copy-start.2
  49.1 13.7 %collective-permute-start = (bf16[1,64,16,128]{3,2,1,0:T(8,128)(2,1)}, bf16[1,64,16,128]{3,2,1,0:T(8,128)(2,1)}, u32[]{:S(2)}, u32[]{:S(2)}) collective-permute-start(bf16[1,64,16,128]{3,2,1,0:T(8,128)(2,1)} %bitcast.9), channel_id=1, source_target_pairs={{0,2},{2,4},{4,6},{6,8},{8,10},{10,12},{12,14},{1,3},{3,5},{5,7},{... | collective-permute-start | bytes 786440 | tf_op jit(solution)/shard_map/ppermute | solution.py:14
  53.2 9.6 %collective-permute-start.1 = (bf16[1,64,16,128]{3,2,1,0:T(8,128)(2,1)}, bf16[1,64,16,128]{3,2,1,0:T(8,128)(2,1)}, u32[]{:S(2)}, u32[]{:S(2)}) collective-permute-start(bf16[1,64,16,128]{3,2,1,0:T(8,128)(2,1)} %bitcast.11), channel_id=1, source_target_pairs={{2,0},{4,2},{6,4},{8,6},{10,8},{12,10},{14,12},{3,1},{5,3},{7,5},{... | collective-permute-start | bytes 786440 | tf_op jit(solution)/shard_map/ppermute | solution.py:15
  66.7 0.7 copy-start.6
  85.2 0.7 copy-start.4
  85.2 64.4 %reduce-scatter.5.cloned.1.call-start = ((), (), s32[]{:S(2)}) async-start(), calls=%async_computation.4 | async-start | bytes 6291456 | tf_op jit(solution)/shard_map/reduce_scatter | solution.py:45
  99.8 15.3 %collective-permute-start.2 = (bf16[1,64,16,128]{3,1,2,0:T(8,128)(2,1)S(1)}, bf16[1,64,16,128]{3,1,2,0:T(8,128)(2,1)S(1)}, u32[]{:S(2)}, u32[]{:S(2)}) collective-permute-start(bf16[1,64,16,128]{3,1,2,0:T(8,128)(2,1)S(1)} %get-tuple-element.5), channel_id=1, source_target_pairs={{0,2},{2,4},{4,6},{6,8},{8,10},{10,12},{12,14},{1,3},{3,5},{5,7},{... | collective-permute-start | bytes 786440 | tf_op jit(solution)/shard_map/ppermute | solution.py:14
  103.5 11.5 %collective-permute-start.3 = (bf16[1,64,16,128]{3,1,2,0:T(8,128)(2,1)S(1)}, bf16[1,64,16,128]{3,1,2,0:T(8,128)(2,1)S(1)}, u32[]{:S(2)}, u32[]{:S(2)}) collective-permute-start(bf16[1,64,16,128]{3,1,2,0:T(8,128)(2,1)S(1)} %get-tuple-element.6), channel_id=1, source_target_pairs={{2,0},{4,2},{6,4},{8,6},{10,8},{12,10},{14,12},{3,1},{5,3},{7,5},{... | collective-permute-start | bytes 786440 | tf_op jit(solution)/shard_map/ppermute | solution.py:15
  115.6 2.0 %copy-start.3 = (bf16[3,3,3,256,256]{4,3,2,1,0:T(8,128)(2,1)S(1)}, bf16[3,3,3,256,256]{4,3,2,1,0:T(8,128)(2,1)}, u32[]{:S(2)}) copy-start(bf16[3,3,3,256,256]{4,3,2,1,0:T(8,128)(2,1)} %param.8) | copy-start | bytes 10616836
  135.5 0.7 copy-start.5
  136.2 17.0 %copy-start.1 = (bf16[3,3,3,256,256]{4,3,2,1,0:T(8,128)(2,1)S(1)}, bf16[3,3,3,256,256]{4,3,2,1,0:T(8,128)(2,1)}, u32[]{:S(2)}) copy-start(bf16[3,3,3,256,256]{4,3,2,1,0:T(8,128)(2,1)} %param.6) | copy-start | bytes 10616836
Sparse Core Ops, SparseCore 0:
  85.3 12.4 reduce-scatter.2
  135.6 13.8 reduce-scatter.4
